TPU v7x, 32 devices: a whole 2x2x4 slice. The times are simulated.
32 devices in a mesh: rhombus: 4 (over z), tile: 8 (over y, x, core).
Axes of the slice: x: 2, y: 2, z: 4, core: 2. Of those that a mesh axis runs over, the one named last changes fastest.
Arguments:
- fine_latent: bfloat16 [16384, 512], P(('rhombus', 'tile')), may hold values from -6 to 6
- mid_latent: bfloat16 [1024, 512], P(('rhombus', 'tile')), may hold values from -6 to 6
- coarse_latent: bfloat16 [642, 512], replicated, may hold values from -6 to 6
- fine_parent: int32 [16384], P(('rhombus', 'tile')), may hold values from 0 to 95, as said below
- mid_parent: int32 [1024], P(('rhombus', 'tile')), may hold values from 0 to 641
- halo_rows: int32 [8192], P(('rhombus', 'tile')), may hold values from 0 to 511
- edge_source: int32 [98304], P(('rhombus', 'tile')), may hold values from 0 to 767
- edge_target: int32 [98304], P(('rhombus', 'tile')), may hold values from 0 to 512, as said below
- w_child: bfloat16 [512, 512], replicated, may hold values from -1 to 1
- mid_w1: bfloat16 [512, 512], replicated, may hold values from -0.25 to 0.25
- mid_w2: bfloat16 [512, 512], replicated, may hold values from -0.5 to 0.5
- mid_w3: bfloat16 [512, 512], replicated, may hold values from -0.25 to 0.25
- w_coarse: bfloat16 [512, 512], replicated, may hold values from -1 to 1
- coarse_w1: bfloat16 [512, 512], replicated, may hold values from -0.25 to 0.25
- coarse_w2: bfloat16 [512, 512], replicated, may hold values from -0.5 to 0.5
- coarse_w3: bfloat16 [512, 512], replicated, may hold values from -0.25 to 0.25
- w_descend: bfloat16 [512, 512], replicated, may hold values from -0.25 to 0.25
- w_fine: bfloat16 [512, 512], replicated, may hold values from -0.25 to 0.25
- edge_w_src: bfloat16 [512, 512], replicated, may hold values from -1 to 1
- edge_w_dst: bfloat16 [512, 512], replicated, may hold values from -0.25 to 0.25
- edge_w2: bfloat16 [512, 512], replicated, may hold values from -0.25 to 0.25
- node_w1: bfloat16 [512, 512], replicated, may hold values from -0.25 to 0.25
- node_w2: bfloat16 [512, 512], replicated, may hold values from -0.125 to 0.125
- node_w3: bfloat16 [512, 512], replicated, may hold values from -0.25 to 0.25
Outputs:
- fine_out: bfloat16 [16384, 512], P(('rhombus', 'tile'))
- mid_out: bfloat16 [1024, 512], P(('rhombus', 'tile'))
- coarse_out: bfloat16 [642, 512], replicated
Inputs may be any that keep to these rules, and one draw needn't show every extreme that they name: `fine_parent`: in tile t of a group, an entry p < 32 names a middle slot of the same tile, 32 <= p < 64 a slot of tile t - 1, 64 <= p a slot of tile t + 1; tile 0 never names the tile before and the last tile of a group never names the tile after. `edge_target`: in each tile the live slots come first and name a fine row of that tile; the remaining slots hold 512. Each tile has at least 1536 live slots, and some tile has all 3072 slots live.
All inputs are finite; a program needn't handle non-finite values.
Results may differ from a plain program's by a relative error of at most 0.013.
Values may be sent and summed in bfloat16 or wider, within the bound.
A program may use at most 64 MiB of HBM per device.

v0:
```python
import jax
import jax.numpy as jnp
from jax import lax
from jax.sharding import PartitionSpec as P

EPSILON = 1e-05


def extended_2(shard, sides, width):
    for axis, dim in sides:
        size, length = (lax.axis_size(axis), shard.shape[dim])
        up = [(i, (i + 1) % size) for i in range(size - 1)]
        down = [(j, i) for i, j in up]
        last = lax.slice_in_dim(shard, length - width, length, axis=dim)
        leading = lax.slice_in_dim(shard, 0, width, axis=dim)
        before = lax.ppermute(last, axis, up)
        after = lax.ppermute(leading, axis, down)
        shard = jnp.concatenate([before, shard, after], axis=dim)
    return shard


def product(left, right):
    return jnp.dot(left, right, preferred_element_type=jnp.float32)


def normed(values):
    return values / jnp.sqrt(jnp.mean(values * values, axis=-1, keepdims=True) + EPSILON)


def node_update(latent, incoming, first, second, third):
    hidden = jax.nn.silu(product(latent, first) + product(incoming, second)).astype(jnp.bfloat16)
    return (latent.astype(jnp.float32) + normed(product(hidden, third))).astype(jnp.bfloat16)


def coarse_update(latent, incoming, coarse_w1, coarse_w2, coarse_w3, w_descend):
    updated = node_update(latent, incoming.astype(jnp.bfloat16), coarse_w1, coarse_w2, coarse_w3)
    return (updated, product(updated, w_descend).astype(jnp.bfloat16))


def selector_rows(row_ids, width):
    columns = lax.broadcasted_iota(jnp.int32, (row_ids.shape[0], width), 1)
    return (columns == row_ids[:, None]).astype(jnp.bfloat16)


def edge_update(
    node_table, lifted, source, target, edge_w_src, edge_w_dst, edge_w2, node_w1, node_w2, node_w3
):
    fine_count = lifted.shape[0]
    sender = product(node_table, edge_w_src).astype(jnp.bfloat16)
    receiver = product(lifted, edge_w_dst).astype(jnp.bfloat16)
    source_pick = selector_rows(source, node_table.shape[0])
    target_pick = selector_rows(target, fine_count)
    edge_sum = product(source_pick, sender) + product(target_pick, receiver)
    edge_hidden = jax.nn.silu(edge_sum).astype(jnp.bfloat16)
    hidden_sums = lax.dot_general(
        target_pick, edge_hidden, (((0,), (0,)), ((), ())), preferred_element_type=jnp.float32
    )
    aggregate = jnp.dot(hidden_sums, edge_w2.astype(jnp.float32), precision=lax.Precision.HIGHEST)
    return node_update(lifted, aggregate.astype(jnp.bfloat16), node_w1, node_w2, node_w3)


def on_device(
    fine_latent,
    mid_latent,
    coarse_latent,
    fine_parent,
    mid_parent,
    halo_rows,
    edge_source,
    edge_target,
    w_child,
    mid_w1,
    mid_w2,
    mid_w3,
    w_coarse,
    coarse_w1,
    coarse_w2,
    coarse_w3,
    w_descend,
    w_fine,
    edge_w_src,
    edge_w_dst,
    edge_w2,
    node_w1,
    node_w2,
    node_w3,
):
    fine_count = fine_latent.shape[0]
    mid_count = mid_latent.shape[0]
    coarse_count = coarse_latent.shape[0]
    rim_count = halo_rows.shape[0] // 2
    child_msg = product(fine_latent, w_child).astype(jnp.bfloat16)
    slot_ids = lax.broadcasted_iota(jnp.int32, (3 * mid_count, fine_count), 0)
    picker = (slot_ids == fine_parent[None, :]).astype(jnp.bfloat16)
    partial_sums = product(picker, child_msg)
    extended = extended_2(partial_sums[mid_count:], (("tile", 0),), mid_count)
    mid_in = partial_sums[:mid_count] + extended[:mid_count] + extended[3 * mid_count :]
    mid_up = node_update(mid_latent, mid_in.astype(jnp.bfloat16), mid_w1, mid_w2, mid_w3)
    mid_msg = product(mid_up, w_coarse).astype(jnp.bfloat16)
    coarse_ids = lax.broadcasted_iota(jnp.int32, (coarse_count, mid_count), 0)
    selector = (coarse_ids == mid_parent[None, :]).astype(jnp.bfloat16)
    coarse_in = lax.psum(product(selector, mid_msg), ("rhombus", "tile"))
    coarse_out, down_coarse = coarse_update(
        coarse_latent, coarse_in, coarse_w1, coarse_w2, coarse_w3, w_descend
    )
    lookup = selector_rows(mid_parent, coarse_count)
    mid_out = (mid_up.astype(jnp.float32) + product(lookup, down_coarse)).astype(jnp.bfloat16)
    fine_down = product(mid_out, w_fine).astype(jnp.bfloat16)
    nearby = extended_2(fine_down, (("tile", 0),), mid_count)
    remapped = jnp.where(
        fine_parent < mid_count,
        fine_parent + mid_count,
        jnp.where(fine_parent < 2 * mid_count, fine_parent - mid_count, fine_parent),
    )
    parent_pick = selector_rows(remapped, 3 * mid_count)
    lifted = (fine_latent.astype(jnp.float32) + product(parent_pick, nearby)).astype(jnp.bfloat16)
    boundary = product(selector_rows(halo_rows, fine_count), lifted).astype(jnp.bfloat16)
    bordered = extended_2(boundary, (("tile", 0),), rim_count)
    node_table = jnp.concatenate([lifted, bordered[:rim_count], bordered[3 * rim_count :]], axis=0)
    fine_out = edge_update(
        node_table,
        lifted,
        edge_source,
        edge_target,
        edge_w_src,
        edge_w_dst,
        edge_w2,
        node_w1,
        node_w2,
        node_w3,
    )
    return (fine_out, mid_out, coarse_out)


def solution(mesh):
    placed = (
        P(("rhombus", "tile"), None),
        P(("rhombus", "tile"), None),
        P(),
        P(("rhombus", "tile")),
        P(("rhombus", "tile")),
        P(("rhombus", "tile")),
        P(("rhombus", "tile")),
        P(("rhombus", "tile")),
        P(),
        P(),
        P(),
        P(),
        P(),
        P(),
        P(),
        P(),
        P(),
        P(),
        P(),
        P(),
        P(),
        P(),
        P(),
        P(),
    )
    return jax.shard_map(
        on_device,
        mesh=mesh,
        in_specs=placed,
        out_specs=(P(("rhombus", "tile"), None), P(("rhombus", "tile"), None), P()),
        check_vma=False,
    )
```

profile of v0, /device:TPU:1, one launch (start us, length us, event | category | flops | bytes accessed | tf_op | source)
XLA Modules:
  0.0 112.6 jit_solution(14659364361576790947)
XLA Ops:
  0.6 0.0 copy-start
  0.7 1.9 %fusion.9 = f32[96,512]{1,0:T(8,128)S(1)} fusion(bf16[512,512]{1,0:T(8,128)(2,1)} %param.24, bf16[512,512]{1,0:T(8,128)(2,1)} %param.32, s32[512]{0:T(512)} %param.27), kind=kOutput, calls=%fused_computation.23 | convolution fusion | flops 319078400 | bytes 1247232 | tf_op jit(solution)/shard_map/dot_general | solution.py:23
  2.6 0.0 copy-start.6
  2.7 4.6 %collective-permute-start = (f32[32,512]{1,0:T(8,128)S(1)}, f32[32,512]{1,0:T(8,128)S(1)}, u32[]{:S(2)}, u32[]{:S(2)}) collective-permute-start(f32[32,512]{1,0:T(8,128)S(1)} %get-tuple-element.5), channel_id=1, source_target_pairs={{0,1},{1,2},{2,3},{3,4},{4,5},{5,6},{6,7},{8,9},{9,10},{10,11},{11... | collective-permute-start | bytes 196616 | tf_op jit(solution)/shard_map/ppermute | solution.py:16
  7.3 1.9 %collective-permute-start.1 = (f32[32,512]{1,0:T(8,128)S(1)}, f32[32,512]{1,0:T(8,128)S(1)}, u32[]{:S(2)}, u32[]{:S(2)}) collective-permute-start(f32[32,512]{1,0:T(8,128)S(1)} %get-tuple-element.6), channel_id=1, source_target_pairs={{1,0},{2,1},{3,2},{4,3},{5,4},{6,5},{7,6},{9,8},{10,9},{11,10},{12... | collective-permute-start | bytes 196616 | tf_op jit(solution)/shard_map/ppermute | solution.py:17
  9.2 1.6 %fusion.51 = f32[642,512]{1,0:T(8,128)} fusion(bf16[642,512]{1,0:T(8,128)(2,1)S(1)} %copy-done.1, bf16[512,512]{1,0:T(8,128)(2,1)S(1)} %copy-done.3), kind=kOutput, calls=%fused_computation.80 | convolution fusion | flops 336592896 | bytes 2496512 | tf_op jit(solution)/shard_map/dot_general | solution.py:23
  10.9 0.2 fusion.50
  11.1 1.8 %collective-permute-done.1 = f32[32,512]{1,0:T(8,128)S(1)} collective-permute-done((f32[32,512]{1,0:T(8,128)S(1)}, f32[32,512]{1,0:T(8,128)S(1)}, u32[]{:S(2)}, u32[]{:S(2)}) %collective-permute-start.1) | collective-permute-done | bytes 65568 | tf_op jit(solution)/shard_map/ppermute | solution.py:17
  12.9 0.5 multiply_reduce_fusion.2
  13.4 0.1 add_convert_fusion.2
  13.5 0.5 fusion.12
  14.0 54.2 %all-reduce.1 = bf16[642,512]{1,0:T(8,128)(2,1)S(1)} all-reduce(f32[642,512]{1,0:T(8,128)S(1)} %fusion.12), channel_id=1, replica_groups=mesh['rhombus'=4,'tile'=8] {'rhombus','tile'}, use_global_device_ids=true, to_apply=%region_1.2 | all-reduce | flops 328704 | bytes 1972224 | tf_op jit(solution)/shard_map/psum | solution.py:102
  68.3 2.8 %multiply_reduce_fusion = (f32[642]{0:T(1024)S(1)}, f32[642,512]{1,0:T(8,128)S(1)}) fusion(bf16[512,512]{1,0:T(8,128)(2,1)} %param.39, f32[642,512]{1,0:T(8,128)} %fusion.51, bf16[512,512]{1,0:T(8,128)(2,1)} %param.38, bf16[642,512]{1,0:T(8,128)(2,1)S(1)} %all-reduce.1), kind=kOutput, calls=%fused_computation.15 | convolution fusion | flops 675814784 | bytes 4338184 | tf_op jit(solution)/shard_map/dot_general | solution.py:23
  71.0 0.3 add_convert_fusion
  71.4 2.0 %fusion.11 = bf16[32,512]{1,0:T(8,128)(2,1)S(1)} fusion(bf16[642,512]{1,0:T(8,128)(2,1)S(1)} %add_convert_fusion, bf16[512,512]{1,0:T(8,128)(2,1)} %param.40, bf16[32,512]{1,0:T(8,128)(2,1)S(1)} %add_convert_fusion.2, s32[32]{0:T(128)S(1)} %copy-done.14), kind=kOutput, calls=%fused_computation.27 | convolution fusion | flops 358028352 | bytes 1247360 | tf_op jit(solution)/shard_map/dot_general | solution.py:23
  73.4 0.2 convolution_convert_fusion.6
  73.5 4.6 %collective-permute-start.2 = (bf16[32,512]{1,0:T(8,128)(2,1)S(1)}, bf16[32,512]{1,0:T(8,128)(2,1)S(1)}, u32[]{:S(2)}, u32[]{:S(2)}) collective-permute-start(bf16[32,512]{1,0:T(8,128)(2,1)S(1)} %convolution_convert_fusion.6), channel_id=1, source_target_pairs={{0,1},{1,2},{2,3},{3,4},{4,5},{5,6},{6,7},{8,9},{9,10},{10,11},{11... | collective-permute-start | bytes 98312 | tf_op jit(solution)/shard_map/ppermute | solution.py:16
  78.1 1.9 %collective-permute-start.3 = (bf16[32,512]{1,0:T(8,128)(2,1)S(1)}, bf16[32,512]{1,0:T(8,128)(2,1)S(1)}, u32[]{:S(2)}, u32[]{:S(2)}) collective-permute-start(bf16[32,512]{1,0:T(8,128)(2,1)S(1)} %convolution_convert_fusion.6), channel_id=1, source_target_pairs={{1,0},{2,1},{3,2},{4,3},{5,4},{6,5},{7,6},{9,8},{10,9},{11,10},{12... | collective-permute-start | bytes 98312 | tf_op jit(solution)/shard_map/ppermute | solution.py:17
  80.1 3.3 %collective-permute-done.3 = bf16[32,512]{1,0:T(8,128)(2,1)S(1)} collective-permute-done((bf16[32,512]{1,0:T(8,128)(2,1)S(1)}, bf16[32,512]{1,0:T(8,128)(2,1)S(1)}, u32[]{:S(2)}, u32[]{:S(2)}) %collective-permute-start.3) | collective-permute-done | bytes 32800 | tf_op jit(solution)/shard_map/ppermute | solution.py:17
  83.4 0.4 fusion.6
  83.8 0.3 convolution_convert_fusion.5
  84.1 1.9 %collective-permute-start.4 = (bf16[128,512]{1,0:T(8,128)(2,1)S(1)}, bf16[128,512]{1,0:T(8,128)(2,1)}, u32[]{:S(2)}, u32[]{:S(2)}) collective-permute-start(bf16[128,512]{1,0:T(8,128)(2,1)S(1)} %get-tuple-element.3), channel_id=1, source_target_pairs={{0,1},{1,2},{2,3},{3,4},{4,5},{5,6},{6,7},{8,9},{9,10},{10,11},{11... | collective-permute-start | bytes 393224 | tf_op jit(solution)/shard_map/ppermute | solution.py:16
  86.1 3.3 %collective-permute-start.5 = (bf16[128,512]{1,0:T(8,128)(2,1)S(1)}, bf16[128,512]{1,0:T(8,128)(2,1)}, u32[]{:S(2)}, u32[]{:S(2)}) collective-permute-start(bf16[128,512]{1,0:T(8,128)(2,1)S(1)} %get-tuple-element.4), channel_id=1, source_target_pairs={{1,0},{2,1},{3,2},{4,3},{5,4},{6,5},{7,6},{9,8},{10,9},{11,10},{12... | collective-permute-start | bytes 393224 | tf_op jit(solution)/shard_map/ppermute | solution.py:17
  89.5 4.8 %fusion.2 = f32[3072,512]{1,0:T(8,128)} fusion(s32[3072]{0:T(1024)S(1)} %copy-done.16, bf16[512,512]{1,0:T(8,128)(2,1)S(1)} %fusion.6, bf16[512,512]{1,0:T(8,128)(2,1)S(1)} %copy-done), kind=kOutput, calls=%fused_computation.5 | convolution fusion | flops 1880883200 | bytes 7352320 | tf_op jit(solution)/shard_map/dot_general | solution.py:23
  94.3 0.4 fusion.52
  94.7 0.6 copy-done.15
  95.3 2.5 %convolution_convert_fusion = bf16[768,512]{1,0:T(8,128)(2,1)} fusion(bf16[512,512]{1,0:T(8,128)(2,1)S(1)} %copy-done.15, bf16[128,512]{1,0:T(8,128)(2,1)} %collective-permute-done.5, bf16[128,512]{1,0:T(8,128)(2,1)} %collective-permute-done.4, bf16[512,512]{1,0:T(8,128)(2,1)S(1)} %fusion.6), kind=kOutput, calls=%fused_computation.10 | convolution fusion | flops 405405696 | bytes 2097152 | tf_op jit(solution)/shard_map/dot_general | solution.py:23
  97.8 8.3 %fusion.1 = f32[512,512]{1,0:T(8,128)S(1)} fusion(s32[3072]{0:T(1024)S(1)} %copy-done.16, f32[3072,512]{1,0:T(8,128)} %fusion.2, bf16[768,512]{1,0:T(8,128)(2,1)} %convolution_convert_fusion, s32[3072]{0:T(1024)S(1)} %copy-done.17), kind=kOutput, calls=%fused_computation.4 | convolution fusion | flops 4039901184 | bytes 8151040 | tf_op jit(solution)/shard_map/dot_general | solution.py:55
  106.0 2.8 %convolution_convert_fusion.4 = bf16[512,512]{1,0:T(8,128)(2,1)} fusion(f32[512,512]{1,0:T(8,128)S(1)} %fusion.1, bf16[512,512]{1,0:T(8,128)(2,1)} %param.44), kind=kOutput, calls=%fused_computation.20 | convolution fusion | flops 1610874880 | bytes 2097152 | tf_op jit(solution)/shard_map/dot_general | solution.py:58
  108.9 2.4 %multiply_reduce_fusion.1 = (f32[512]{0:T(512)S(1)}, f32[512,512]{0,1:T(8,128)S(1)}) fusion(bf16[512,512]{1,0:T(8,128)(2,1)} %param.47, f32[512,512]{1,0:T(8,128)S(1)} %fusion.52, bf16[512,512]{1,0:T(8,128)(2,1)} %convolution_convert_fusion.4, bf16[512,512]{1,0:T(8,128)(2,1)} %param.46), kind=kOutput, calls=%fused_computation.32 | convolution fusion | flops 538967552 | bytes 3672064 | tf_op jit(solution)/shard_map/dot_general | solution.py:23
  111.3 0.3 copy.27
  111.6 1.0 add_convert_fusion.1
  (45 shorter events, 0.2 us)
Async XLA Ops:
  0.6 88.8 %copy-start = (bf16[512,512]{1,0:T(8,128)(2,1)S(1)}, bf16[512,512]{1,0:T(8,128)(2,1)}, u32[]{:S(2)}) copy-start(bf16[512,512]{1,0:T(8,128)(2,1)} %param.43) | copy-start | bytes 1572868
  0.6 8.6 %copy-start.1 = (bf16[642,512]{1,0:T(8,128)(2,1)S(1)}, bf16[642,512]{1,0:T(8,128)(2,1)}, u32[]{:S(2)}) copy-start(bf16[642,512]{1,0:T(8,128)(2,1)} %param.26) | copy-start | bytes 1972228
  0.7 8.6 %copy-start.3 = (bf16[512,512]{1,0:T(8,128)(2,1)S(1)}, bf16[512,512]{1,0:T(8,128)(2,1)}, u32[]{:S(2)}) copy-start(bf16[512,512]{1,0:T(8,128)(2,1)} %param.37) | copy-start | bytes 1572868
  2.6 8.3 %copy-start.6 = (bf16[512,512]{1,0:T(8,128)(2,1)S(1)}, bf16[512,512]{1,0:T(8,128)(2,1)}, u32[]{:S(2)}) copy-start(bf16[512,512]{1,0:T(8,128)(2,1)} %param.33) | copy-start | bytes 1572868
  2.6 8.2 %copy-start.11 = (bf16[32,512]{1,0:T(8,128)(2,1)S(1)}, bf16[32,512]{1,0:T(8,128)(2,1)}, u32[]{:S(2)}) copy-start(bf16[32,512]{1,0:T(8,128)(2,1)} %param.25) | copy-start | bytes 98308
  2.6 10.2 %copy-start.4 = (bf16[512,512]{1,0:T(8,128)(2,1)S(1)}, bf16[512,512]{1,0:T(8,128)(2,1)}, u32[]{:S(2)}) copy-start(bf16[512,512]{1,0:T(8,128)(2,1)} %param.35) | copy-start | bytes 1572868
  2.7 10.2 %copy-start.5 = (bf16[512,512]{1,0:T(8,128)(2,1)S(1)}, bf16[512,512]{1,0:T(8,128)(2,1)}, u32[]{:S(2)}) copy-start(bf16[512,512]{1,0:T(8,128)(2,1)} %param.34) | copy-start | bytes 1572868
  2.7 8.4 %collective-permute-start = (f32[32,512]{1,0:T(8,128)S(1)}, f32[32,512]{1,0:T(8,128)S(1)}, u32[]{:S(2)}, u32[]{:S(2)}) collective-permute-start(f32[32,512]{1,0:T(8,128)S(1)} %get-tuple-element.5), channel_id=1, source_target_pairs={{0,1},{1,2},{2,3},{3,4},{4,5},{5,6},{6,7},{8,9},{9,10},{10,11},{11... | collective-permute-start | bytes 196616 | tf_op jit(solution)/shard_map/ppermute | solution.py:16
  7.3 5.6 %collective-permute-start.1 = (f32[32,512]{1,0:T(8,128)S(1)}, f32[32,512]{1,0:T(8,128)S(1)}, u32[]{:S(2)}, u32[]{:S(2)}) collective-permute-start(f32[32,512]{1,0:T(8,128)S(1)} %get-tuple-element.6), channel_id=1, source_target_pairs={{1,0},{2,1},{3,2},{4,3},{5,4},{6,5},{7,6},{9,8},{10,9},{11,10},{12... | collective-permute-start | bytes 196616 | tf_op jit(solution)/shard_map/ppermute | solution.py:17
  10.9 2.6 %copy-start.9 = (bf16[512,512]{1,0:T(8,128)(2,1)S(1)}, bf16[512,512]{1,0:T(8,128)(2,1)}, u32[]{:S(2)}) copy-start(bf16[512,512]{1,0:T(8,128)(2,1)} %param.36) | copy-start | bytes 1572868
  10.9 2.6 %copy-start.14 = (s32[32]{0:T(128)S(1)}, s32[32]{0:T(128)}, u32[]{:S(2)}) copy-start(s32[32]{0:T(128)} %param.28) | copy-start | bytes 388
  71.3 12.4 %copy-start.2 = (bf16[642,512]{1,0:T(8,128)(2,1)}, bf16[642,512]{1,0:T(8,128)(2,1)S(1)}, u32[]{:S(2)}) copy-start(bf16[642,512]{1,0:T(8,128)(2,1)S(1)} %add_convert_fusion) | copy-start | bytes 1972228
  71.3 2.0 %copy-start.7 = (bf16[512,512]{1,0:T(8,128)(2,1)S(1)}, bf16[512,512]{1,0:T(8,128)(2,1)}, u32[]{:S(2)}) copy-start(bf16[512,512]{1,0:T(8,128)(2,1)} %param.41) | copy-start | bytes 1572868
  71.3 8.8 %copy-start.13 = (s32[512]{0:T(512)S(1)}, s32[512]{0:T(512)}, u32[]{:S(2)}) copy-start(s32[512]{0:T(512)} %param.27) | copy-start | bytes 6148
  71.3 12.0 %copy-start.8 = (bf16[512,512]{1,0:T(8,128)(2,1)S(1)}, bf16[512,512]{1,0:T(8,128)(2,1)}, u32[]{:S(2)}) copy-start(bf16[512,512]{1,0:T(8,128)(2,1)} %param.24) | copy-start | bytes 1572868
  71.3 12.4 %copy-start.18 = (s32[256]{0:T(256)S(1)}, s32[256]{0:T(256)}, u32[]{:S(2)}) copy-start(s32[256]{0:T(256)} %param.29) | copy-start | bytes 3076
  73.3 20.9 %copy-start.12 = (bf16[32,512]{1,0:T(8,128)(2,1)}, bf16[32,512]{1,0:T(8,128)(2,1)S(1)}, u32[]{:S(2)}) copy-start(bf16[32,512]{1,0:T(8,128)(2,1)S(1)} %fusion.11) | copy-start | bytes 98308
  73.3 16.1 %copy-start.16 = (s32[3072]{0:T(1024)S(1)}, s32[3072]{0:T(1024)}, u32[]{:S(2)}) copy-start(s32[3072]{0:T(1024)} %param.31) | copy-start | bytes 36868
  73.5 6.6 %collective-permute-start.2 = (bf16[32,512]{1,0:T(8,128)(2,1)S(1)}, bf16[32,512]{1,0:T(8,128)(2,1)S(1)}, u32[]{:S(2)}, u32[]{:S(2)}) collective-permute-start(bf16[32,512]{1,0:T(8,128)(2,1)S(1)} %convolution_convert_fusion.6), channel_id=1, source_target_pairs={{0,1},{1,2},{2,3},{3,4},{4,5},{5,6},{6,7},{8,9},{9,10},{10,11},{11... | collective-permute-start | bytes 98312 | tf_op jit(solution)/shard_map/ppermute | solution.py:16
  78.1 5.2 %collective-permute-start.3 = (bf16[32,512]{1,0:T(8,128)(2,1)S(1)}, bf16[32,512]{1,0:T(8,128)(2,1)S(1)}, u32[]{:S(2)}, u32[]{:S(2)}) collective-permute-start(bf16[32,512]{1,0:T(8,128)(2,1)S(1)} %convolution_convert_fusion.6), channel_id=1, source_target_pairs={{1,0},{2,1},{3,2},{4,3},{5,4},{6,5},{7,6},{9,8},{10,9},{11,10},{12... | collective-permute-start | bytes 98312 | tf_op jit(solution)/shard_map/ppermute | solution.py:17
  84.1 10.6 %collective-permute-start.4 = (bf16[128,512]{1,0:T(8,128)(2,1)S(1)}, bf16[128,512]{1,0:T(8,128)(2,1)}, u32[]{:S(2)}, u32[]{:S(2)}) collective-permute-start(bf16[128,512]{1,0:T(8,128)(2,1)S(1)} %get-tuple-element.3), channel_id=1, source_target_pairs={{0,1},{1,2},{2,3},{3,4},{4,5},{5,6},{6,7},{8,9},{9,10},{10,11},{11... | collective-permute-start | bytes 393224 | tf_op jit(solution)/shard_map/ppermute | solution.py:16
  86.1 8.2 %copy-start.10 = (bf16[512,512]{1,0:T(8,128)(2,1)S(1)}, bf16[512,512]{1,0:T(8,128)(2,1)}, u32[]{:S(2)}) copy-start(bf16[512,512]{1,0:T(8,128)(2,1)} %param.45) | copy-start | bytes 1572868
  86.1 8.6 %collective-permute-start.5 = (bf16[128,512]{1,0:T(8,128)(2,1)S(1)}, bf16[128,512]{1,0:T(8,128)(2,1)}, u32[]{:S(2)}, u32[]{:S(2)}) collective-permute-start(bf16[128,512]{1,0:T(8,128)(2,1)S(1)} %get-tuple-element.4), channel_id=1, source_target_pairs={{1,0},{2,1},{3,2},{4,3},{5,4},{6,5},{7,6},{9,8},{10,9},{11,10},{12... | collective-permute-start | bytes 393224 | tf_op jit(solution)/shard_map/ppermute | solution.py:17
  94.3 1.0 copy-start.15
  94.7 3.1 %copy-start.17 = (s32[3072]{0:T(1024)S(1)}, s32[3072]{0:T(1024)}, u32[]{:S(2)}) copy-start(s32[3072]{0:T(1024)} %param.30) | copy-start | bytes 36868
where the time goes:
time: 113 us
  blocking collectives  54.2 us (48%)
  matrix products  31.5 us (28%)
  starting transfers between devices  18.3 us (16%)
  waiting for transfers between devices  5.11 us (5%)
  other arithmetic  1.4 us (1%)
    psum x1, blocking collectives, on_device(): coarse_in = lax.psum(product(selector, mid_msg), ('rhombus', 'tile'))  54.2 us
    dot_general x14, matrix products, product(): return jnp.dot(left, right, preferred_element_type=jnp.float32)  20.4 us
    ppermute x3, starting transfers between devices, extended_2(): before = lax.ppermute(last, axis, up)  11.1 us
    dot_general x1, matrix products, edge_update(): lax.dot_general(target_pick, edge_hidden, (((0,), (0,)), ((), ())), prefe...  8.28 us
    ppermute x3, starting transfers between devices, extended_2(): after = lax.ppermute(leading, axis, down)  7.19 us
    ppermute x3, waiting for transfers between devices, extended_2(): after = lax.ppermute(leading, axis, down)  5.11 us
    dot_general x1, matrix products, edge_update(): jnp.dot(hidden_sums, edge_w2.astype(jnp.float32), precision=lax.Precision...  2.83 us
  transfers between devices with their start and end apart: 6, of which 2 were waited for; matrix products, arithmetic and copies ran while one was open for 6% of the time, Pallas kernels for 0%

commit v1 on v0

--- a/solution.py
+++ b/solution.py
@@ -99,7 +99,9 @@
     mid_msg = product(mid_up, w_coarse).astype(jnp.bfloat16)
     coarse_ids = lax.broadcasted_iota(jnp.int32, (coarse_count, mid_count), 0)
     selector = (coarse_ids == mid_parent[None, :]).astype(jnp.bfloat16)
-    coarse_in = lax.psum(product(selector, mid_msg), ("rhombus", "tile"))
+    block = product(selector, mid_msg)
+    parts = lax.all_gather(block, ("rhombus", "tile"), axis=0, tiled=False)
+    coarse_in = parts.sum(axis=0)
     coarse_out, down_coarse = coarse_update(
         coarse_latent, coarse_in, coarse_w1, coarse_w2, coarse_w3, w_descend
     )

time: 113 us -> 327 us (2.89)
  waiting for transfers between devices: 5.11 us -> 244 us
  blocking collectives: 54.2 us -> 0 us
  other arithmetic: 1.4 us -> 19.6 us
  between operations: 1.03 us -> 14.4 us
    all_gather x0 -> x1, waiting for transfers between devices: none -> 238 us  [on_device(): parts = lax.all_gather(block, ('rhombus', 'tile'), axis=0, tiled=False)]
    psum x1 -> x0, blocking collectives: 54.2 us -> none  [on_device(): coarse_in = lax.psum(product(selector, mid_msg), ('rhombus', 'tile'))]
    reduce_sum x0 -> x1, other arithmetic: none -> 16.8 us  [on_device(): coarse_in = parts.sum(axis=0)]
  transfers between devices with their start and end apart: 6 -> 7, of which waited for: 2 -> 3; matrix products, arithmetic and copies ran while one was open for 6% -> 2% of each run, Pallas kernels for 0% -> 0%
where the time goes in v1:
time: 327 us; the launch traced here: 326 us
  waiting for transfers between devices  244 us (75%)
  matrix products  29.9 us (9%)
  other arithmetic  19.6 us (6%)
  starting transfers between devices  16.2 us (5%)
  between operations  14.4 us (4%)
    all_gather x1, waiting for transfers between devices, on_device(): parts = lax.all_gather(block, ('rhombus', 'tile'), axis=0, tiled=False)  238 us
    dot_general x14, matrix products, product(): return jnp.dot(left, right, preferred_element_type=jnp.float32)  19.8 us
    reduce_sum x1, other arithmetic, on_device(): coarse_in = parts.sum(axis=0)  16.8 us
    ppermute x3, starting transfers between devices, extended_2(): before = lax.ppermute(last, axis, up)  9.62 us
    dot_general x1, matrix products, edge_update(): lax.dot_general(target_pick, edge_hidden, (((0,), (0,)), ((), ())), prefe...  8.33 us
    ppermute x3, waiting for transfers between devices, extended_2(): after = lax.ppermute(leading, axis, down)  6.72 us
    ppermute x3, starting transfers between devices, extended_2(): after = lax.ppermute(leading, axis, down)  6.56 us
  transfers between devices with their start and end apart: 7, of which 3 were waited for; matrix products, arithmetic and copies ran while one was open for 2% of the time, Pallas kernels for 0%

profile of v1, /device:TPU:1, one launch (start us, length us, event | category | flops | bytes accessed | tf_op | source)
XLA Modules:
  0.0 326.2 jit_solution(4855994777211288693)
XLA Ops:
  7.3 1.9 fusion.9
  9.2 4.5 %collective-permute-start = (f32[32,512]{1,0:T(8,128)S(1)}, f32[32,512]{1,0:T(8,128)S(1)}, u32[]{:S(2)}, u32[]{:S(2)}) collective-permute-start(f32[32,512]{1,0:T(8,128)S(1)} %get-tuple-element.5), channel_id=1, source_target_pairs={{0,1},{1,2},{2,3},{3,4},{4,5},{5,6},{6,7},{8,9},{9,10},{10,11},{11... | collective-permute-start | bytes 196616 | tf_op jit(solution)/shard_map/ppermute | solution.py:16
  13.7 1.9 collective-permute-start.1
  15.7 0.2 fusion.49
  15.9 3.4 %collective-permute-done.1 = f32[32,512]{1,0:T(8,128)S(1)} collective-permute-done((f32[32,512]{1,0:T(8,128)S(1)}, f32[32,512]{1,0:T(8,128)S(1)}, u32[]{:S(2)}, u32[]{:S(2)}) %collective-permute-start.1) | collective-permute-done | bytes 65568 | tf_op jit(solution)/shard_map/ppermute | solution.py:17
  19.3 0.5 multiply_reduce_fusion.2
  19.8 0.1 add_convert_fusion.2
  20.0 2.8 convolution_bitcast_fusion
  22.8 0.5 fusion.50
  23.3 237.7 %all-gather.4.cloned.1.call-done = f32[32,642,512]{2,1,0:T(8,128)} async-done(((f32[1,642,512]{2,1,0:T(8,128)}), f32[32,642,512]{2,1,0:T(8,128)}) %all-gather.4.cloned.1.call-update) | async-done | bytes 42074128 | tf_op jit(solution)/shard_map/all_gather | solution.py:103
  261.0 16.8 %reduce_sum.37 = bf16[642,512]{1,0:T(8,128)(2,1)S(1)} reduce(f32[32,642,512]{2,1,0:T(8,128)} %all-gather.4.cloned.1.call-done, f32[]{:T(128)} %constant.15.clone.1), dimensions={0}, to_apply=%region_1.2 | reduce | flops 10189824 | bytes 42731524 | tf_op jit(solution)/shard_map/reduce_sum | solution.py:104
  277.8 3.3 %multiply_reduce_fusion = (f32[642]{0:T(1024)S(1)}, f32[642,512]{1,0:T(8,128)}) fusion(bf16[512,512]{1,0:T(8,128)(2,1)} %param.39, f32[642,512]{1,0:T(8,128)S(1)} %fusion.50, bf16[512,512]{1,0:T(8,128)(2,1)} %param.38, bf16[642,512]{1,0:T(8,128)(2,1)S(1)} %reduce_sum.37), kind=kOutput, calls=%fused_computation.16 | convolution fusion | flops 675814784 | bytes 4338184 | tf_op jit(solution)/shard_map/dot_general | solution.py:23
  281.1 1.6 add_convert_fusion
  282.9 0.6 fusion.11
  283.5 0.6 copy-done.8
  284.1 0.2 convolution_convert_fusion.6
  284.3 3.2 collective-permute-start.2
  287.5 1.9 collective-permute-start.3
  289.5 3.3 %collective-permute-done.3 = bf16[32,512]{1,0:T(8,128)(2,1)S(1)} collective-permute-done((bf16[32,512]{1,0:T(8,128)(2,1)S(1)}, bf16[32,512]{1,0:T(8,128)(2,1)S(1)}, u32[]{:S(2)}, u32[]{:S(2)}) %collective-permute-start.3) | collective-permute-done | bytes 32800 | tf_op jit(solution)/shard_map/ppermute | solution.py:17
  292.7 0.3 fusion.6
  293.1 0.3 convolution_convert_fusion.5
  293.5 1.9 collective-permute-start.4
  295.4 2.7 collective-permute-start.5
  298.2 4.8 %fusion.2 = f32[3072,512]{1,0:T(8,128)} fusion(s32[3072]{0:T(1024)S(1)} %copy-done.18, bf16[512,512]{1,0:T(8,128)(2,1)S(1)} %fusion.6, bf16[512,512]{1,0:T(8,128)(2,1)S(1)} %copy-done), kind=kOutput, calls=%fused_computation.5 | convolution fusion | flops 1880883200 | bytes 7352320 | tf_op jit(solution)/shard_map/dot_general | solution.py:23
  303.0 0.4 fusion.51
  303.5 0.6 copy-done.17
  304.0 1.5 convolution_convert_fusion
  305.5 8.3 %fusion.1 = f32[512,512]{1,0:T(8,128)S(1)} fusion(s32[3072]{0:T(1024)S(1)} %copy-done.18, f32[3072,512]{1,0:T(8,128)} %fusion.2, bf16[768,512]{1,0:T(8,128)(2,1)} %convolution_convert_fusion, s32[3072]{0:T(1024)S(1)} %copy-done.19), kind=kOutput, calls=%fused_computation.4 | convolution fusion | flops 4039901184 | bytes 8151040 | tf_op jit(solution)/shard_map/dot_general | solution.py:55
  313.8 1.8 convolution_convert_fusion.4
  315.6 2.4 multiply_reduce_fusion.1
  318.0 0.3 copy.28
  318.4 1.0 add_convert_fusion.1
  (52 shorter events, 0.2 us)
Async XLA Ops:
  7.2 291.0 %copy-start = (bf16[512,512]{1,0:T(8,128)(2,1)S(1)}, bf16[512,512]{1,0:T(8,128)(2,1)}, u32[]{:S(2)}) copy-start(bf16[512,512]{1,0:T(8,128)(2,1)} %param.43) | copy-start | bytes 1572868
  7.2 8.5 %copy-start.12 = (bf16[32,512]{1,0:T(8,128)(2,1)S(1)}, bf16[32,512]{1,0:T(8,128)(2,1)}, u32[]{:S(2)}) copy-start(bf16[32,512]{1,0:T(8,128)(2,1)} %param.25) | copy-start | bytes 98308
  7.2 8.5 %copy-start.7 = (bf16[512,512]{1,0:T(8,128)(2,1)S(1)}, bf16[512,512]{1,0:T(8,128)(2,1)}, u32[]{:S(2)}) copy-start(bf16[512,512]{1,0:T(8,128)(2,1)} %param.33) | copy-start | bytes 1572868
  7.2 12.1 %copy-start.5 = (bf16[512,512]{1,0:T(8,128)(2,1)S(1)}, bf16[512,512]{1,0:T(8,128)(2,1)}, u32[]{:S(2)}) copy-start(bf16[512,512]{1,0:T(8,128)(2,1)} %param.34) | copy-start | bytes 1572868
  7.2 12.1 %copy-start.4 = (bf16[512,512]{1,0:T(8,128)(2,1)S(1)}, bf16[512,512]{1,0:T(8,128)(2,1)}, u32[]{:S(2)}) copy-start(bf16[512,512]{1,0:T(8,128)(2,1)} %param.35) | copy-start | bytes 1572868
  7.2 253.7 %all-gather.4.cloned.1.call-start = ((), (), s32[]{:S(2)}) async-start(), calls=%async_computation | async-start | bytes 43794432 | tf_op jit(solution)/shard_map/all_gather | solution.py:103
  9.2 10.7 %copy-start.15 = (s32[32]{0:T(128)S(1)}, s32[32]{0:T(128)}, u32[]{:S(2)}) copy-start(s32[32]{0:T(128)} %param.28) | copy-start | bytes 388
  9.2 6.6 %collective-permute-start = (f32[32,512]{1,0:T(8,128)S(1)}, f32[32,512]{1,0:T(8,128)S(1)}, u32[]{:S(2)}, u32[]{:S(2)}) collective-permute-start(f32[32,512]{1,0:T(8,128)S(1)} %get-tuple-element.5), channel_id=1, source_target_pairs={{0,1},{1,2},{2,3},{3,4},{4,5},{5,6},{6,7},{8,9},{9,10},{10,11},{11... | collective-permute-start | bytes 196616 | tf_op jit(solution)/shard_map/ppermute | solution.py:16
  13.7 5.6 %collective-permute-start.1 = (f32[32,512]{1,0:T(8,128)S(1)}, f32[32,512]{1,0:T(8,128)S(1)}, u32[]{:S(2)}, u32[]{:S(2)}) collective-permute-start(f32[32,512]{1,0:T(8,128)S(1)} %get-tuple-element.6), channel_id=1, source_target_pairs={{1,0},{2,1},{3,2},{4,3},{5,4},{6,5},{7,6},{9,8},{10,9},{11,10},{12... | collective-permute-start | bytes 196616 | tf_op jit(solution)/shard_map/ppermute | solution.py:17
  19.9 2.8 copy-start.2
  20.0 2.8 copy-start.6
  281.1 1.7 copy-start.16
  282.8 10.3 %copy-start.3 = (bf16[642,512]{1,0:T(8,128)(2,1)}, bf16[642,512]{1,0:T(8,128)(2,1)S(1)}, u32[]{:S(2)}) copy-start(bf16[642,512]{1,0:T(8,128)(2,1)S(1)} %add_convert_fusion) | copy-start | bytes 1972228
  282.8 1.3 copy-start.8
  282.8 6.6 %copy-start.14 = (s32[512]{0:T(512)S(1)}, s32[512]{0:T(512)}, u32[]{:S(2)}) copy-start(s32[512]{0:T(512)} %param.27) | copy-start | bytes 6148
  282.9 9.9 %copy-start.9 = (bf16[512,512]{1,0:T(8,128)(2,1)S(1)}, bf16[512,512]{1,0:T(8,128)(2,1)}, u32[]{:S(2)}) copy-start(bf16[512,512]{1,0:T(8,128)(2,1)} %param.24) | copy-start | bytes 1572868
  282.9 10.2 %copy-start.20 = (s32[256]{0:T(256)S(1)}, s32[256]{0:T(256)}, u32[]{:S(2)}) copy-start(s32[256]{0:T(256)} %param.29) | copy-start | bytes 3076
  284.1 18.9 %copy-start.13 = (bf16[32,512]{1,0:T(8,128)(2,1)}, bf16[32,512]{1,0:T(8,128)(2,1)S(1)}, u32[]{:S(2)}) copy-start(bf16[32,512]{1,0:T(8,128)(2,1)S(1)} %fusion.11) | copy-start | bytes 98308
  284.1 14.1 %copy-start.18 = (s32[3072]{0:T(1024)S(1)}, s32[3072]{0:T(1024)}, u32[]{:S(2)}) copy-start(s32[3072]{0:T(1024)} %param.31) | copy-start | bytes 36868
  284.3 5.2 %collective-permute-start.2 = (bf16[32,512]{1,0:T(8,128)(2,1)S(1)}, bf16[32,512]{1,0:T(8,128)(2,1)S(1)}, u32[]{:S(2)}, u32[]{:S(2)}) collective-permute-start(bf16[32,512]{1,0:T(8,128)(2,1)S(1)} %convolution_convert_fusion.6), channel_id=1, source_target_pairs={{0,1},{1,2},{2,3},{3,4},{4,5},{5,6},{6,7},{8,9},{9,10},{10,11},{11... | collective-permute-start | bytes 98312 | tf_op jit(solution)/shard_map/ppermute | solution.py:16
  287.5 5.2 %collective-permute-start.3 = (bf16[32,512]{1,0:T(8,128)(2,1)S(1)}, bf16[32,512]{1,0:T(8,128)(2,1)S(1)}, u32[]{:S(2)}, u32[]{:S(2)}) collective-permute-start(bf16[32,512]{1,0:T(8,128)(2,1)S(1)} %convolution_convert_fusion.6), channel_id=1, source_target_pairs={{1,0},{2,1},{3,2},{4,3},{5,4},{6,5},{7,6},{9,8},{10,9},{11,10},{12... | collective-permute-start | bytes 98312 | tf_op jit(solution)/shard_map/ppermute | solution.py:17
  293.5 9.9 %collective-permute-start.4 = (bf16[128,512]{1,0:T(8,128)(2,1)S(1)}, bf16[128,512]{1,0:T(8,128)(2,1)S(1)}, u32[]{:S(2)}, u32[]{:S(2)}) collective-permute-start(bf16[128,512]{1,0:T(8,128)(2,1)S(1)} %get-tuple-element.3), channel_id=1, source_target_pairs={{0,1},{1,2},{2,3},{3,4},{4,5},{5,6},{6,7},{8,9},{9,10},{10,11},{11... | collective-permute-start | bytes 393224 | tf_op jit(solution)/shard_map/ppermute | solution.py:16
  295.4 7.5 %copy-start.10 = (bf16[512,512]{1,0:T(8,128)(2,1)S(1)}, bf16[512,512]{1,0:T(8,128)(2,1)}, u32[]{:S(2)}) copy-start(bf16[512,512]{1,0:T(8,128)(2,1)} %param.45) | copy-start | bytes 1572868
  295.4 8.0 %collective-permute-start.5 = (bf16[128,512]{1,0:T(8,128)(2,1)S(1)}, bf16[128,512]{1,0:T(8,128)(2,1)S(1)}, u32[]{:S(2)}, u32[]{:S(2)}) collective-permute-start(bf16[128,512]{1,0:T(8,128)(2,1)S(1)} %get-tuple-element.4), channel_id=1, source_target_pairs={{1,0},{2,1},{3,2},{4,3},{5,4},{6,5},{7,6},{9,8},{10,9},{11,10},{12... | collective-permute-start | bytes 393224 | tf_op jit(solution)/shard_map/ppermute | solution.py:17
  303.0 1.0 copy-start.17
  303.4 2.1 copy-start.19
  305.5 8.3 %copy-start.11 = (bf16[512,512]{1,0:T(8,128)(2,1)S(1)}, bf16[512,512]{1,0:T(8,128)(2,1)}, u32[]{:S(2)}) copy-start(bf16[512,512]{1,0:T(8,128)(2,1)} %param.44) | copy-start | bytes 1572868
  318.0 1.4 copy-start.1
Sparse Core Ops, SparseCore 0:
  22.9 238.0 all-gather.3
